TPU v7x, 128 devices: a whole 4x4x4 slice. The times are simulated.
128 devices in a mesh: dp: 8 (over z_lo, y), sp: 16 (over x, z_hi, core).
Axes of the slice: x: 4, y: 4, z: 4 (z_hi: 2, z_lo: 2; z = z_hi * 2 + z_lo), core: 2. Of those that a mesh axis runs over, the one named last changes fastest.
Arguments:
- feats: bfloat16 [8, 32, 256, 128], P('dp', None, 'sp'), may hold values from -62 to 62
- conv_w: bfloat16 [1152, 256], replicated, may hold values from -0.1875 to 0.1875
- group_norm_gain: float32 [256], replicated, may hold values from 0.5 to 1.5
- group_norm_bias: float32 [256], replicated, may hold values from -3 to 3
- emb_w: bfloat16 [256, 3072], replicated, may hold values from -0.375 to 0.375
- time_w: bfloat16 [256, 9216], replicated, may hold values from -0.375 to 0.375
- up_w: bfloat16 [3072, 6144], P(None, 'sp'), may hold values from -0.109375 to 0.109375
- down_w: bfloat16 [6144, 3072], P('sp'), may hold values from -0.078125 to 0.078125
- steps: int32 [8], P('dp'), may hold values from 0 to 999
- cotangent: bfloat16 [8, 2048, 3072], P('dp', 'sp'), may hold values from -28 to 28
Outputs:
- grad_conv: float32 [1152, 256], replicated
- grad_up: float32 [3072, 6144], P('dp', 'sp')
- grad_down: float32 [6144, 3072], P('sp', 'dp')
All inputs are finite; a program needn't handle non-finite values.
Results may differ from a plain program's by a relative error of at most 0.012.
Values may be sent and summed in bfloat16 or wider, within the bound.
A program may use at most 192 MiB of HBM per device.

v0:
```python
import math
import jax
import jax.numpy as jnp
from jax import lax
from jax.sharding import Mesh
from jax.sharding import PartitionSpec as P

NORM_GROUPS = 32
SP = ("sp_0", "sp_1", "sp_2")
DP_SP = ("dp", "sp_0", "sp_1", "sp_2")


def from_behind(array, axis, by):
    length = lax.axis_size(axis)
    pairs = [(i, i + by) for i in range(length) if 0 <= i + by < length]
    return lax.ppermute(array, axis, pairs)


def copy_for_each(array, axis):
    length = lax.axis_size(axis)
    return lax.all_to_all(
        jnp.broadcast_to(array[None], (length, *array.shape)), axis, 0, 0, tiled=True
    )


def over_copies(array, axis):
    return copy_for_each(array, axis).sum(axis=0)


def in_one(arrays, axis):
    ends = [0]
    for a in arrays:
        ends.append(ends[-1] + a.size)
    subtotal = over_copies(jnp.concatenate([a.ravel() for a in arrays]), axis)
    return tuple((subtotal[b:e].reshape(a.shape) for a, b, e in zip(arrays, ends, ends[1:])))


def side_by_side(arrays, axis, dim, along):
    both = jnp.concatenate(arrays, axis=along)
    filled, at, finished = (lax.all_gather(both, axis, axis=dim, tiled=True), 0, [])
    for a in arrays:
        finished.append(lax.slice_in_dim(filled, at, at + a.shape[along], axis=along))
        at += a.shape[along]
    return tuple(finished)


def in_blocks(array, dim, length):
    before, after = (array.shape[:dim], array.shape[dim + 1 :])
    return jnp.moveaxis(array.reshape(*before, length, -1, *after), dim, 0)


def sum_by_chip(array, chips, core, dim):
    sizes = (lax.axis_size(chips), lax.axis_size(core))
    parts = in_blocks(array, dim, sizes[0] * sizes[1])
    inside = parts.shape[1:]
    parts = parts.reshape(*sizes, *inside).swapaxes(0, 1).reshape(-1, *inside)
    parts = lax.psum_scatter(parts, core, scatter_dimension=0, tiled=True)
    return lax.psum_scatter(parts, chips, scatter_dimension=0, tiled=True)[0]


def sum_packed(arrays, axis, dims):
    length = lax.axis_size(axis)
    parts = [in_blocks(a, dim, length) for a, dim in zip(arrays, dims)]
    lines = jnp.concatenate([b.reshape(length, -1) for b in parts], axis=1)
    rows = max(16, -(-lines.shape[1] // 1024) * 8)
    lines = jnp.pad(lines, ((0, 0), (0, rows * 128 - lines.shape[1]))).reshape(-1, 128)
    ravelled, at, finished = (lax.psum_scatter(lines, axis, tiled=True).reshape(-1), 0, [])
    for b in parts:
        part = b[0]
        finished.append(ravelled[at : at + part.size].reshape(part.shape))
        at += part.size
    return tuple(finished)


def gelu_pair(u):
    coef = math.sqrt(2.0 / math.pi)
    inner = coef * (u + 0.044715 * u * u * u)
    tangent = jnp.tanh(inner)
    value = 0.5 * u * (1.0 + tangent)
    slope = 0.5 * (1.0 + tangent) + 0.5 * u * (1.0 - tangent * tangent) * coef * (
        1.0 + 3.0 * 0.044715 * u * u
    )
    return (value, slope)


def silu_pair(value):
    sigma = jax.nn.sigmoid(value)
    return (value * sigma, sigma * (1.0 + value * (1.0 - sigma)))


def modulation(step_value, time_w):
    half = time_w.shape[0] // 2
    freqs = jnp.exp(-math.log(10000.0) * jnp.arange(half, dtype=jnp.float32) / half)
    angle = step_value.astype(jnp.float32) * freqs
    embed = jnp.concatenate([jnp.cos(angle), jnp.sin(angle)])
    mixed = jnp.dot(
        jax.nn.silu(embed).astype(jnp.bfloat16)[None, :], time_w, preferred_element_type=jnp.float32
    )[0]
    width = time_w.shape[1] // 3
    return (mixed[:width], mixed[width : 2 * width], mixed[2 * width :])


def make_patches(padded, rows, cols):
    pieces = []
    for row_tap in range(3):
        for col_tap in range(3):
            pieces.append(
                padded[row_tap : row_tap + 2 * rows : 2, col_tap : col_tap + 2 * cols : 2, :]
            )
    stacked = jnp.concatenate(pieces, axis=-1)
    return stacked.reshape(rows * cols, stacked.shape[-1])


def group_totals(first, second, groups):
    tokens, width = first.shape
    first_g = first.reshape(tokens, groups, width // groups)
    second_g = second.reshape(tokens, groups, width // groups)
    return (jnp.sum(first_g, axis=(0, 2)), jnp.sum(second_g, axis=(0, 2)))


def broadcast_groups(values, width):
    return jnp.repeat(values, width // values.shape[0])


def contract(left, right, left_dim, right_dim):
    return lax.dot_general(
        left, right, (((left_dim,), (right_dim,)), ((), ())), preferred_element_type=jnp.float32
    )


def on_device(
    feats, conv_w, group_norm_gain, group_norm_bias, emb_w, time_w, up_w, down_w, steps, cotangent
):
    devices_sp = lax.axis_size(SP)
    image = feats[0]
    rows_in, cols_in, _ = image.shape
    rows = rows_in // 2
    cols = cols_in // 2
    seq_rows = rows // devices_sp
    channel_count = conv_w.shape[1]
    rim = from_behind(image[:, cols_in - 1, :], SP, 1)
    widened = jnp.concatenate([rim[:, None, :], image], axis=1)
    padded = jnp.pad(widened, ((1, 0), (0, 0), (0, 0)))
    patches = make_patches(padded, rows, cols)
    normed_value = jnp.dot(patches, conv_w, preferred_element_type=jnp.float32)
    first, second = group_totals(normed_value, normed_value * normed_value, NORM_GROUPS)
    first, second = in_one((first, second), SP)
    group_count = normed_value.shape[0] * devices_sp * (channel_count // NORM_GROUPS)
    group_mean = first / group_count
    rstd = lax.rsqrt(second / group_count - group_mean * group_mean + 1e-05)
    channel_rstd = broadcast_groups(rstd, channel_count)
    centered_input = (normed_value - broadcast_groups(group_mean, channel_count)) * channel_rstd
    preactivation = centered_input * group_norm_gain + group_norm_bias
    act_val, silu_slope = silu_pair(preactivation)
    act_b = act_val.astype(jnp.bfloat16)
    shift, scale, gate = modulation(steps[0], time_w)
    cot_seq = cotangent[0]
    moved = lax.all_to_all(
        act_b.reshape(rows, cols, channel_count), SP, split_axis=0, concat_axis=1, tiled=True
    )
    local_act = moved.reshape(seq_rows * cols * devices_sp, channel_count)
    hidden_in = jnp.dot(local_act, emb_w, preferred_element_type=jnp.float32)
    centered = hidden_in - jnp.mean(hidden_in, axis=-1, keepdims=True)
    token_rstd = lax.rsqrt(jnp.mean(centered * centered, axis=-1, keepdims=True) + 1e-06)
    hhat = centered * token_rstd
    normed = (hhat * (1.0 + scale) + shift).astype(jnp.bfloat16)
    all_normed, all_cot = side_by_side((normed, cot_seq), SP, 0, 1)
    upper = jnp.dot(all_normed, up_w, preferred_element_type=jnp.float32)
    gelu_val, gelu_slope = gelu_pair(upper)
    hid = gelu_val.astype(jnp.bfloat16)
    scaled_cot = (all_cot.astype(jnp.float32) * gate).astype(jnp.bfloat16)
    dhid = contract(scaled_cot, down_w, 1, 1)
    dupper = (dhid * gelu_slope).astype(jnp.bfloat16)
    dnormed = sum_by_chip(
        contract(dupper, up_w, 1, 1).astype(jnp.bfloat16), ("sp_0", "sp_1"), "sp_2", 0
    ).astype(jnp.float32)
    grad_up_local = contract(all_normed, dupper, 0, 0)
    grad_down_local = contract(hid, scaled_cot, 0, 0)
    grad_up, grad_down = tuple(
        (
            part.astype(jnp.float32)
            for part in sum_packed(
                (grad_up_local.astype(jnp.bfloat16), grad_down_local.astype(jnp.bfloat16)),
                "dp",
                (0, 1),
            )
        )
    )
    dhh = dnormed * (1.0 + scale)
    dhh_mean = jnp.mean(dhh, axis=-1, keepdims=True)
    dhh_cross = jnp.mean(dhh * hhat, axis=-1, keepdims=True)
    dh_val = (
        cot_seq.astype(jnp.float32) + token_rstd * (dhh - dhh_mean - hhat * dhh_cross)
    ).astype(jnp.bfloat16)
    dact = contract(dh_val, emb_w, 1, 1)
    back_tiles = lax.all_to_all(
        dact.reshape(seq_rows, cols * devices_sp, channel_count).astype(jnp.bfloat16),
        SP,
        split_axis=1,
        concat_axis=0,
        tiled=True,
    ).astype(jnp.float32)
    dact_tile = back_tiles.reshape(rows * cols, channel_count)
    input_gradient = dact_tile * silu_slope * group_norm_gain
    backward_first, backward_second = group_totals(
        input_gradient, input_gradient * centered_input, NORM_GROUPS
    )
    backward_first, backward_second = in_one((backward_first, backward_second), SP)
    normed_gradient = (
        channel_rstd
        * (
            input_gradient
            - broadcast_groups(backward_first / group_count, channel_count)
            - centered_input * broadcast_groups(backward_second / group_count, channel_count)
        )
    ).astype(jnp.bfloat16)
    conv_local = contract(patches, normed_gradient, 0, 0)
    grad_conv = lax.psum(conv_local, DP_SP)
    return (grad_conv, grad_up, grad_down)


def solution(mesh):
    finer = Mesh(mesh.devices.reshape(mesh.shape["dp"], 4, 2, 2), ("dp", "sp_0", "sp_1", "sp_2"))
    in_specs = (
        P("dp", None, SP, None),
        P(),
        P(),
        P(),
        P(),
        P(),
        P(None, SP),
        P(SP, None),
        P("dp"),
        P("dp", SP, None),
    )
    out_specs = (P(), P("dp", SP), P(SP, "dp"))
    return jax.shard_map(
        on_device, mesh=finer, in_specs=in_specs, out_specs=out_specs, check_vma=False
    )
```

profile of v0, /device:TPU:1, one launch (start us, length us, event | category | flops | bytes accessed | tf_op | source)
XLA Modules:
  0.0 589.0 jit_solution(9743201290991420241)
XLA Ops:
  7.2 1.1 copy.52
  8.3 6.9 %collective-permute-start = (bf16[32,128]{1,0:T(8,128)(2,1)S(1)}, bf16[32,128]{1,0:T(8,128)(2,1)S(1)}, u32[]{:S(2)}, u32[]{:S(2)}) collective-permute-start(bf16[32,128]{1,0:T(8,128)(2,1)S(1)} %slice_bitcast_fusion), channel_id=1, source_target_pairs={{0,1},{1,2},{2,3},{3,4},{4,5},{5,6},{6,7},{7,8},{8,9},{9,10},{10,1... | collective-permute-start | bytes 24584 | tf_op jit(solution)/shard_map/ppermute | solution.py:16
  16.0 0.2 slice.74
  16.2 0.2 slice.73
  16.5 0.3 slice.72
  16.8 0.2 slice.71
  17.0 0.2 slice.70
  17.2 0.3 slice.69
  17.6 0.2 slice.68
  17.8 0.2 slice.67
  18.0 0.4 slice.75
  18.6 1.3 fusion.62
  20.1 0.1 reduce_sum.120
  20.2 0.1 reduce_sum.123
  20.4 0.6 broadcast_in_dim.15
  21.0 7.9 %all-to-all-start = ((f32[16,1,64]{2,1,0:T(1,128)}), f32[16,1,64]{2,1,0:T(1,128)S(1)}, u32[]{:S(2)}, u32[]{:S(2)}) async-start(f32[16,1,64]{2,1,0:T(1,128)} %broadcast_in_dim.15), calls=%async_computation | async-start | bytes 16384 | tf_op jit(solution)/shard_map/all_to_all | solution.py:21
  29.0 3.1 fusion.66
  32.0 3.9 all-to-all-done
  36.1 0.1 sub.52
  36.2 0.1 mul.175
  36.3 0.7 fusion.52
  37.0 4.0 all-to-all-start.1
  41.0 7.4 %all-to-all-done.1 = bf16[16,8,256]{2,1,0:T(8,128)(2,1)S(1)} async-done(((bf16[16,8,256]{2,1,0:T(8,128)(2,1)}), bf16[16,8,256]{2,1,0:T(8,128)(2,1)S(1)}, u32[]{:S(2)}, u32[]{:S(2)}) %all-to-all-start.1) | async-done | bytes 65568 | tf_op jit(solution)/shard_map/all_to_all | solution.py:158
  48.4 1.9 fusion.65
  50.4 0.3 multiply_reduce_fusion
  50.7 0.9 copy-done.2
  51.6 0.3 add_convert_fusion
  51.9 1.3 pad_maximum_fusion.1
  53.3 0.2 reduce-scatter.4.cloned.1.call-start
  53.5 146.6 %all-gather.2.cloned.1.call-done = bf16[2048,6144]{1,0:T(8,128)(2,1)} async-done(((bf16[128,6144]{1,0:T(8,128)(2,1)}), bf16[2048,6144]{1,0:T(8,128)(2,1)}) %all-gather.2.cloned.1.call-update) | async-done | bytes 25165840 | tf_op jit(solution)/shard_map/all_gather | solution.py:40
  200.1 9.7 %fusion.2 = f32[2048,384]{1,0:T(8,128)S(1)} fusion(bf16[3072,384]{1,0:T(8,128)(2,1)S(1)} %copy-done, bf16[2048,6144]{1,0:T(8,128)(2,1)} %all-gather.2.cloned.1.call-done), kind=kOutput, calls=%fused_computation.4 | convolution fusion | flops 4831838208 | bytes 18087936 | tf_op jit(solution)/shard_map/dot_general | solution.py:168
  209.9 12.3 %fusion.16 = bf16[2048,384]{1,0:T(8,128)(2,1)S(1)} fusion(f32[2048,384]{1,0:T(8,128)S(1)} %fusion.2, bf16[384,3072]{1,0:T(8,128)(2,1)S(1)} %copy-done.8, bf16[2048,6144]{1,0:T(8,128)(2,1)} %all-gather.2.cloned.1.call-done, f32[3072]{0:T(1024)S(1)} %get-tuple-element.12), kind=kOutput, calls=%fused_computation.19 | convolution fusion | flops 4865654784 | bytes 19673088 | tf_op jit(solution)/shard_map/dot_general | solution.py:126
  222.2 7.0 %convolution_convert_fusion = bf16[2048,3072]{1,0:T(8,128)(2,1)S(1)} fusion(bf16[2048,384]{1,0:T(8,128)(2,1)S(1)} %fusion.16, bf16[3072,384]{1,0:T(8,128)(2,1)S(1)} %copy-done), kind=kOutput, calls=%fused_computation.1 | convolution fusion | flops 4838129664 | bytes 16515072 | tf_op jit(solution)/shard_map/dot_general | solution.py:126
  229.3 5.4 copy.33
  234.6 0.3 reduce-scatter.6.cloned.1.call-start
  234.9 1.1 copy-done.10
  236.0 10.8 %fusion.7 = bf16[3072,384]{1,0:T(8,128)(2,1)} fusion(bf16[2048,384]{1,0:T(8,128)(2,1)S(1)} %copy-done.10, bf16[2048,6144]{1,0:T(8,128)(2,1)} %all-gather.2.cloned.1.call-done), kind=kOutput, calls=%fused_computation.12 | convolution fusion | flops 4833017856 | bytes 16515072 | tf_op jit(solution)/shard_map/dot_general | solution.py:126
  246.8 3.2 reshape_reshape.7
  250.0 13.4 %fusion.6 = bf16[384,3072]{1,0:T(8,128)(2,1)S(1)} fusion(bf16[2048,6144]{1,0:T(8,128)(2,1)} %all-gather.2.cloned.1.call-done, f32[3072]{0:T(1024)S(1)} %get-tuple-element.12, f32[2048,384]{1,0:T(8,128)} %copy-done.11), kind=kOutput, calls=%fused_computation.11 | convolution fusion | flops 4858970112 | bytes 18100224 | tf_op jit(solution)/shard_map/dot_general | solution.py:126
  263.4 1.9 copy.37
  265.4 0.3 reduce-scatter.8.cloned.1.call-start
  265.7 10.4 %pad_maximum_fusion = bf16[8,294912]{1,0:T(8,128)(2,1)} fusion(bf16[8,147456]{1,0:T(8,128)(2,1)} %bitcast.67, bf16[8,147456]{1,0:T(8,128)(2,1)S(1)} %reshape_reshape.7), kind=kLoop, calls=%fused_computation.10 | loop fusion | flops 9437184 | bytes 9437184 | tf_op jit(solution)/shard_map/concatenate | solution.py:64
  276.1 6.6 %reshape.118 = bf16[18432,128]{1,0:T(8,128)(2,1)} reshape(bf16[8,294912]{1,0:T(8,128)(2,1)} %pad_maximum_fusion) | data formatting | bytes 9437184 | tf_op jit(solution)/shard_map/reshape | solution.py:66
  282.8 79.5 %reduce-scatter.6.cloned.1.call-done = bf16[1,128,3072]{2,1,0:T(8,128)(2,1)} async-done(((bf16[8,128,3072]{2,1,0:T(8,128)(2,1)}), bf16[1,128,3072]{2,1,0:T(8,128)(2,1)}) %reduce-scatter.6.cloned.1.call-update) | async-done | bytes 786448 | tf_op jit(solution)/shard_map/reduce_scatter | solution.py:58
  362.3 1.6 fusion.19
  364.0 2.5 fusion.29
  366.4 0.1 copy.53
  366.6 0.5 broadcast.119
  367.1 1.0 reduce.10
  368.1 12.2 %all_to_all.30 = bf16[16,2,1024]{2,1,0:T(2,128)(2,1)S(1)} all-to-all(bf16[16,2,1024]{2,1,0:T(2,128)(2,1)S(1)} %reshape.125), channel_id=1, replica_groups=mesh['dp'=8,'sp_0'=4,'sp_1'=2,'sp_2'=2] {'sp_0','sp_1','sp_2'}, dimensions={0} | all-to-all | bytes 131072 | tf_op jit(solution)/shard_map/all_to_all | solution.py:196
  380.4 0.1 fusion.61
  380.5 0.1 reduce_sum.130
  380.6 0.1 reduce_sum.131
  380.8 0.1 reduce_sum.134
  381.0 10.0 %all_to_all.31 = f32[16,1,64]{2,1,0:T(1,128)S(1)} all-to-all(f32[16,1,64]{2,1,0:T(1,128)S(1)} %broadcast_in_dim.18), channel_id=1, replica_groups=mesh['dp'=8,'sp_0'=4,'sp_1'=2,'sp_2'=2] {'sp_0','sp_1','sp_2'}, dimensions={0} | all-to-all | bytes 8192 | tf_op jit(solution)/shard_map/all_to_all | solution.py:21
  391.2 0.1 sub.62
  391.4 0.1 mul.216
  391.5 1.4 fusion.38
  392.9 29.4 %reduce-scatter.8.cloned.1.call-done = bf16[2304,128]{1,0:T(8,128)(2,1)} async-done(((bf16[18432,128]{1,0:T(8,128)(2,1)}), bf16[2304,128]{1,0:T(8,128)(2,1)}) %reduce-scatter.8.cloned.1.call-update) | async-done | bytes 589840 | tf_op jit(solution)/shard_map/reduce_scatter | solution.py:67
  422.3 1.1 slice_convert_fusion
  423.4 1.0 reshape.122
  424.4 1.0 reshape.121
  425.3 154.8 %all-reduce.3.cloned.1.call-done = f32[1152,256]{1,0:T(8,128)} async-done(((f32[1152,256]{1,0:T(8,128)}), f32[1152,256]{1,0:T(8,128)}) %all-reduce.3.cloned.1.call-update) | async-done | bytes 1179664 | tf_op jit(solution)/shard_map/psum | solution.py:218
  580.2 2.4 copy.64
  (66 shorter events, 1.5 us)
Async XLA Ops:
  7.2 193.0 %copy-start = (bf16[3072,384]{1,0:T(8,128)(2,1)S(1)}, bf16[3072,384]{1,0:T(8,128)(2,1)}, u32[]{:S(2)}) copy-start(bf16[3072,384]{1,0:T(8,128)(2,1)} %param.16) | copy-start | bytes 7077892
  8.3 7.7 %collective-permute-start = (bf16[32,128]{1,0:T(8,128)(2,1)S(1)}, bf16[32,128]{1,0:T(8,128)(2,1)S(1)}, u32[]{:S(2)}, u32[]{:S(2)}) collective-permute-start(bf16[32,128]{1,0:T(8,128)(2,1)S(1)} %slice_bitcast_fusion), channel_id=1, source_target_pairs={{0,1},{1,2},{2,3},{3,4},{4,5},{5,6},{6,7},{7,8},{8,9},{9,10},{10,1... | collective-permute-start | bytes 24584 | tf_op jit(solution)/shard_map/ppermute | solution.py:16
  18.5 17.8 %copy-start.6 = (f32[256]{0:T(256)S(1)}, f32[256]{0:T(256)}, u32[]{:S(2)}) copy-start(f32[256]{0:T(256)} %param.13) | copy-start | bytes 3076
  18.5 17.8 %copy-start.7 = (f32[256]{0:T(256)S(1)}, f32[256]{0:T(256)}, u32[]{:S(2)}) copy-start(f32[256]{0:T(256)} %param.12) | copy-start | bytes 3076
  21.0 14.8 %all-to-all-start = ((f32[16,1,64]{2,1,0:T(1,128)}), f32[16,1,64]{2,1,0:T(1,128)S(1)}, u32[]{:S(2)}, u32[]{:S(2)}) async-start(f32[16,1,64]{2,1,0:T(1,128)} %broadcast_in_dim.15), calls=%async_computation | async-start | bytes 16384 | tf_op jit(solution)/shard_map/all_to_all | solution.py:21
  37.0 11.4 %all-to-all-start.1 = ((bf16[16,8,256]{2,1,0:T(8,128)(2,1)}), bf16[16,8,256]{2,1,0:T(8,128)(2,1)S(1)}, u32[]{:S(2)}, u32[]{:S(2)}) async-start(bf16[16,8,256]{2,1,0:T(8,128)(2,1)} %fusion.52), calls=%async_computation.1 | async-start | bytes 131072 | tf_op jit(solution)/shard_map/all_to_all | solution.py:158
  41.0 159.2 %all-gather.2.cloned.1.call-start = ((), (), s32[]{:S(2)}) async-start(), calls=%async_computation.7 | async-start | bytes 26738688 | tf_op jit(solution)/shard_map/all_gather | solution.py:40
  48.4 3.5 copy-start.4
  50.4 1.2 copy-start.2
  53.3 212.1 %reduce-scatter.4.cloned.1.call-start = ((), (), s32[]{:S(2)}) async-start(), calls=%async_computation.8 | async-start | bytes 18874368 | tf_op jit(solution)/shard_map/reduce_scatter | solution.py:57
  200.1 9.8 %copy-start.8 = (bf16[384,3072]{1,0:T(8,128)(2,1)S(1)}, bf16[384,3072]{1,0:T(8,128)(2,1)}, u32[]{:S(2)}) copy-start(bf16[384,3072]{1,0:T(8,128)(2,1)} %param.17) | copy-start | bytes 7077892
  209.9 12.3 %copy-start.11 = (f32[2048,384]{1,0:T(8,128)}, f32[2048,384]{1,0:T(8,128)S(1)}, u32[]{:S(2)}) copy-start(f32[2048,384]{1,0:T(8,128)S(1)} %fusion.2) | copy-start | bytes 9437188
  222.2 7.0 %copy-start.9 = (bf16[2048,384]{1,0:T(8,128)(2,1)}, bf16[2048,384]{1,0:T(8,128)(2,1)S(1)}, u32[]{:S(2)}) copy-start(bf16[2048,384]{1,0:T(8,128)(2,1)S(1)} %fusion.16) | copy-start | bytes 4718596
  234.6 1.4 copy-start.10
  234.6 127.7 %reduce-scatter.6.cloned.1.call-start = ((), (), s32[]{:S(2)}) async-start(), calls=%async_computation.9 | async-start | bytes 7077888 | tf_op jit(solution)/shard_map/reduce_scatter | solution.py:58
  265.4 156.9 %reduce-scatter.8.cloned.1.call-start = ((), (), s32[]{:S(2)}) async-start(), calls=%async_computation.11 | async-start | bytes 5308416 | tf_op jit(solution)/shard_map/reduce_scatter | solution.py:67
  282.7 79.6 %copy-start.3 = (f32[128,3072]{1,0:T(8,128)S(1)}, f32[128,3072]{1,0:T(8,128)}, u32[]{:S(2)}) copy-start(f32[128,3072]{1,0:T(8,128)} %copy-done.2) | copy-start | bytes 4718596
  282.7 81.2 %copy-start.5 = (bf16[1,128,3072]{2,1,0:T(8,128)(2,1)S(1)}, bf16[1,128,3072]{2,1,0:T(8,128)(2,1)}, u32[]{:S(2)}) copy-start(bf16[1,128,3072]{2,1,0:T(8,128)(2,1)} %param.19) | copy-start | bytes 2359300
  282.7 297.4 %all-reduce.3.cloned.1.call-start = ((), (), s32[]{:S(2)}) async-start(), calls=%async_computation.10 | async-start | bytes 2359296 | tf_op jit(solution)/shard_map/psum | solution.py:218
  392.8 189.7 %copy-start.1 = (bf16[3072,384]{1,0:T(8,128)(2,1)S(1)}, bf16[3072,384]{1,0:T(8,128)(2,1)}, u32[]{:S(2)}) copy-start(bf16[3072,384]{1,0:T(8,128)(2,1)} %param.16) | copy-start | bytes 7077892
Sparse Core Ops, SparseCore 0:
  53.4 146.6 all-gather.1
  234.8 21.5 reduce-scatter.3
  265.5 96.7 reduce-scatter.5
  364.7 57.5 reduce-scatter.7
  428.2 151.9 all-reduce.2
where the time goes:
time: 590 us; the launch traced here: 589 us
  waiting for transfers between devices  422 us (72%)
  matrix products  63.3 us (11%)
  local copies, waits for them, and re-layouts  29.3 us (5%)
  blocking collectives  22.2 us (4%)
  starting transfers between devices  19.6 us (3%)
  other arithmetic  17.9 us (3%)
  between operations  14.8 us (3%)
    psum x1, waiting for transfers between devices, on_device(): grad_conv = lax.psum(conv_local, DP_SP)  155 us
    all_gather x1, waiting for transfers between devices, side_by_side(): lax.all_gather(both, axis, axis=dim, tiled=True)  147 us
    reduce_scatter x1, waiting for transfers between devices, sum_by_chip(): return lax.psum_scatter(parts, chips, scatter_dimension=0, tiled=True)[0]  79.5 us
    dot_general x6, matrix products, contract(): lax.dot_general(left, right, (((left_dim,), (right_dim,)), ((), ())), pre...  47.3 us
    reduce_scatter x1, waiting for transfers between devices, sum_packed(): lax.psum_scatter(lines, axis, tiled=True).reshape(-1)  29.4 us
    all_to_all x1, blocking collectives, on_device(): lax.all_to_all(dact.reshape(seq_rows, cols * devices_sp, channel_count).a...  12.2 us
  transfers between devices with their start and end apart: 8, of which 6 were waited for; matrix products, arithmetic and copies ran while one was open for 10% of the time, Pallas kernels for 0%

commit v1 on v0

--- a/solution.py
+++ b/solution.py
@@ -215,7 +215,7 @@
         )
     ).astype(jnp.bfloat16)
     conv_local = contract(patches, normed_gradient, 0, 0)
-    grad_conv = lax.psum(conv_local, DP_SP)
+    grad_conv = jnp.sum(lax.all_gather(conv_local, DP_SP), axis=0)
     return (grad_conv, grad_up, grad_down)
 
 

time: 590 us -> 1300 us (2.20)
  waiting for transfers between devices: 422 us -> 1080 us
  other arithmetic: 17.9 us -> 64.4 us
    all_gather x0 -> x1, waiting for transfers between devices: none -> 818 us  [on_device(): grad_conv = jnp.sum(lax.all_gather(conv_local, DP_SP), axis=0)]
    psum x1 -> x0, waiting for transfers between devices: 155 us -> none  [on_device(): grad_conv = lax.psum(conv_local, DP_SP)]
    reduce_sum x0 -> x1, other arithmetic: none -> 46.5 us  [on_device(): grad_conv = jnp.sum(lax.all_gather(conv_local, DP_SP), axis=0)]
  transfers between devices with their start and end apart: 8 -> 8, of which waited for: 6 -> 6; matrix products, arithmetic and copies ran while one was open for 10% -> 5% of each run, Pallas kernels for 0% -> 0%
where the time goes in v1:
time: 1300 us
  waiting for transfers between devices  1080 us (83%)
  other arithmetic  64.4 us (5%)
  matrix products  63.3 us (5%)
  local copies, waits for them, and re-layouts  26.9 us (2%)
  blocking collectives  22.2 us (2%)
  starting transfers between devices  19.6 us (2%)
  between operations  14.8 us (1%)
    all_gather x1, waiting for transfers between devices, on_device(): grad_conv = jnp.sum(lax.all_gather(conv_local, DP_SP), axis=0)  818 us
    all_gather x1, waiting for transfers between devices, side_by_side(): lax.all_gather(both, axis, axis=dim, tiled=True)  147 us
    reduce_scatter x1, waiting for transfers between devices, sum_by_chip(): return lax.psum_scatter(parts, chips, scatter_dimension=0, tiled=True)[0]  79.6 us
    dot_general x6, matrix products, contract(): lax.dot_general(left, right, (((left_dim,), (right_dim,)), ((), ())), pre...  47.3 us
    reduce_sum x1, other arithmetic, on_device(): grad_conv = jnp.sum(lax.all_gather(conv_local, DP_SP), axis=0)  46.5 us
    reduce_scatter x1, waiting for transfers between devices, sum_packed(): lax.psum_scatter(lines, axis, tiled=True).reshape(-1)  29.4 us
  transfers between devices with their start and end apart: 8, of which 6 were waited for; matrix products, arithmetic and copies ran while one was open for 5% of the time, Pallas kernels for 0%

profile of v1, /device:TPU:1, one launch (start us, length us, event | category | flops | bytes accessed | tf_op | source)
XLA Modules:
  0.0 1296.1 jit_solution(18378264308282329673)
XLA Ops:
  7.2 1.1 copy.52
  8.3 6.9 collective-permute-start
  16.0 0.2 slice.74
  16.2 0.2 slice.73
  16.5 0.3 slice.72
  16.8 0.2 slice.71
  17.0 0.2 slice.70
  17.2 0.3 slice.69
  17.6 0.2 slice.68
  17.8 0.2 slice.67
  18.0 0.4 slice.75
  18.6 1.3 fusion.62
  20.1 0.1 reduce_sum.129
  20.2 0.1 reduce_sum.132
  20.4 0.6 broadcast_in_dim.15
  21.0 7.9 all-to-all-start
  29.0 3.1 fusion.66
  32.0 3.9 all-to-all-done
  36.1 0.1 sub.52
  36.2 0.1 mul.175
  36.3 0.7 fusion.52
  37.0 4.0 all-to-all-start.1
  41.0 7.4 all-to-all-done.1
  48.4 1.9 fusion.65
  50.4 0.3 multiply_reduce_fusion
  50.7 0.9 copy-done.2
  51.6 0.3 add_convert_fusion
  51.9 1.3 pad_maximum_fusion.1
  53.3 0.2 reduce-scatter.4.cloned.1.call-start
  53.5 146.6 %all-gather.4.cloned.1.call-done = bf16[2048,6144]{1,0:T(8,128)(2,1)} async-done(((bf16[128,6144]{1,0:T(8,128)(2,1)}), bf16[2048,6144]{1,0:T(8,128)(2,1)}) %all-gather.4.cloned.1.call-update) | async-done | bytes 25165840 | tf_op jit(solution)/shard_map/all_gather | solution.py:40
  200.1 9.7 fusion.2
  209.9 12.3 fusion.16
  222.2 7.0 convolution_convert_fusion
  229.3 5.4 copy.33
  234.6 0.3 reduce-scatter.6.cloned.1.call-start
  234.9 1.1 copy-done.10
  236.0 10.8 fusion.7
  246.8 3.2 reshape_reshape.7
  250.0 13.4 %fusion.6 = bf16[384,3072]{1,0:T(8,128)(2,1)S(1)} fusion(bf16[2048,6144]{1,0:T(8,128)(2,1)} %all-gather.4.cloned.1.call-done, f32[3072]{0:T(1024)S(1)} %get-tuple-element.12, f32[2048,384]{1,0:T(8,128)} %copy-done.11), kind=kOutput, calls=%fused_computation.11 | convolution fusion | flops 4858970112 | bytes 18100224 | tf_op jit(solution)/shard_map/dot_general | solution.py:126
  263.4 2.0 copy.37
  265.4 0.3 reduce-scatter.8.cloned.1.call-start
  265.7 10.4 pad_maximum_fusion
  276.1 6.6 reshape.118
  282.7 79.6 %reduce-scatter.6.cloned.1.call-done = bf16[1,128,3072]{2,1,0:T(8,128)(2,1)} async-done(((bf16[8,128,3072]{2,1,0:T(8,128)(2,1)}), bf16[1,128,3072]{2,1,0:T(8,128)(2,1)}) %reduce-scatter.6.cloned.1.call-update) | async-done | bytes 786448 | tf_op jit(solution)/shard_map/reduce_scatter | solution.py:58
  362.4 1.6 fusion.19
  364.0 2.5 fusion.29
  366.5 0.1 copy.53
  366.6 0.5 broadcast.119
  367.1 1.0 reduce.10
  368.2 12.2 all_to_all.30
  380.4 0.1 fusion.61
  380.5 0.1 reduce_sum.139
  380.6 0.1 reduce_sum.140
  380.8 0.1 reduce_sum.143
  381.0 10.0 all_to_all.31
  391.2 0.1 sub.62
  391.4 0.1 mul.216
  391.5 1.4 fusion.38
  392.9 29.4 %reduce-scatter.8.cloned.1.call-done = bf16[2304,128]{1,0:T(8,128)(2,1)} async-done(((bf16[18432,128]{1,0:T(8,128)(2,1)}), bf16[2304,128]{1,0:T(8,128)(2,1)}) %reduce-scatter.8.cloned.1.call-update) | async-done | bytes 589840 | tf_op jit(solution)/shard_map/reduce_scatter | solution.py:67
  422.3 1.1 slice_convert_fusion
  423.5 1.0 reshape.122
  424.4 1.0 reshape.121
  425.4 817.7 %all-gather.6.cloned.1.call-done = f32[147456,256]{1,0:T(8,128)} async-done(((f32[1152,256]{1,0:T(8,128)}), f32[147456,256]{1,0:T(8,128)}) %all-gather.6.cloned.1.call-update) | async-done | bytes 150994960 | tf_op jit(solution)/shard_map/all_gather | solution.py:218
  1243.0 46.5 %reduce_sum.145 = f32[1152,256]{1,0:T(8,128)} reduce(f32[128,1152,256]{2,1,0:T(8,128)} %bitcast.17, f32[]{:T(128)} %constant.13.clone.1), dimensions={0}, to_apply=%region_16.17 | reduce | flops 37453824 | bytes 152174592 | tf_op jit(solution)/shard_map/reduce_sum | solution.py:218
  (66 shorter events, 1.5 us)
Async XLA Ops:
  7.2 193.0 %copy-start = (bf16[3072,384]{1,0:T(8,128)(2,1)S(1)}, bf16[3072,384]{1,0:T(8,128)(2,1)}, u32[]{:S(2)}) copy-start(bf16[3072,384]{1,0:T(8,128)(2,1)} %param.16) | copy-start | bytes 7077892
  8.3 7.7 collective-permute-start
  18.5 17.8 %copy-start.6 = (f32[256]{0:T(256)S(1)}, f32[256]{0:T(256)}, u32[]{:S(2)}) copy-start(f32[256]{0:T(256)} %param.13) | copy-start | bytes 3076
  18.5 17.8 %copy-start.7 = (f32[256]{0:T(256)S(1)}, f32[256]{0:T(256)}, u32[]{:S(2)}) copy-start(f32[256]{0:T(256)} %param.12) | copy-start | bytes 3076
  21.0 14.8 %all-to-all-start = ((f32[16,1,64]{2,1,0:T(1,128)}), f32[16,1,64]{2,1,0:T(1,128)S(1)}, u32[]{:S(2)}, u32[]{:S(2)}) async-start(f32[16,1,64]{2,1,0:T(1,128)} %broadcast_in_dim.15), calls=%async_computation | async-start | bytes 16384 | tf_op jit(solution)/shard_map/all_to_all | solution.py:21
  37.0 11.4 all-to-all-start.1
  41.0 159.2 %all-gather.4.cloned.1.call-start = ((), (), s32[]{:S(2)}) async-start(), calls=%async_computation.7 | async-start | bytes 26738688 | tf_op jit(solution)/shard_map/all_gather | solution.py:40
  48.4 3.5 copy-start.4
  50.4 1.2 copy-start.2
  53.3 212.1 %reduce-scatter.4.cloned.1.call-start = ((), (), s32[]{:S(2)}) async-start(), calls=%async_computation.8 | async-start | bytes 18874368 | tf_op jit(solution)/shard_map/reduce_scatter | solution.py:57
  200.1 9.8 copy-start.8
  209.9 12.3 copy-start.11
  222.2 7.0 copy-start.9
  234.6 1.4 copy-start.10
  234.6 127.7 %reduce-scatter.6.cloned.1.call-start = ((), (), s32[]{:S(2)}) async-start(), calls=%async_computation.9 | async-start | bytes 7077888 | tf_op jit(solution)/shard_map/reduce_scatter | solution.py:58
  265.4 156.9 %reduce-scatter.8.cloned.1.call-start = ((), (), s32[]{:S(2)}) async-start(), calls=%async_computation.10 | async-start | bytes 5308416 | tf_op jit(solution)/shard_map/reduce_scatter | solution.py:67
  282.6 79.7 %copy-start.3 = (f32[128,3072]{1,0:T(8,128)S(1)}, f32[128,3072]{1,0:T(8,128)}, u32[]{:S(2)}) copy-start(f32[128,3072]{1,0:T(8,128)} %copy-done.2) | copy-start | bytes 4718596
  282.6 81.3 %copy-start.5 = (bf16[1,128,3072]{2,1,0:T(8,128)(2,1)S(1)}, bf16[1,128,3072]{2,1,0:T(8,128)(2,1)}, u32[]{:S(2)}) copy-start(bf16[1,128,3072]{2,1,0:T(8,128)(2,1)} %param.19) | copy-start | bytes 2359300
  282.7 960.4 %all-gather.6.cloned.1.call-start = ((), (), s32[]{:S(2)}) async-start(), calls=%async_computation.11 | async-start | bytes 152174592 | tf_op jit(solution)/shard_map/all_gather | solution.py:218
  1243.0 46.5 %copy-start.1 = (bf16[3072,384]{1,0:T(8,128)(2,1)S(1)}, bf16[3072,384]{1,0:T(8,128)(2,1)}, u32[]{:S(2)}) copy-start(bf16[3072,384]{1,0:T(8,128)(2,1)} %param.16) | copy-start | bytes 7077892
Sparse Core Ops, SparseCore 0:
  53.4 146.6 all-gather.3
  234.8 21.5 reduce-scatter.3
  265.5 96.7 reduce-scatter.5
  364.7 57.5 reduce-scatter.7
  424.6 818.4 all-gather.5
